TPU v7x, 256 devices: a whole 4x4x8 slice. The times are simulated.
256 devices in a mesh: row: 16 (over x, z_hi, core), col: 16 (over y, z_lo).
Axes of the slice: x: 4, y: 4, z: 8 (z_hi: 2, z_lo: 4; z = z_hi * 4 + z_lo), core: 2. Of those that a mesh axis runs over, the one named last changes fastest.
Arguments:
- amplitudes: bfloat16 [16, 16, 768, 768], P('row', 'col'), may hold values from -0.59765625 to 0.59765625
- ints: bfloat16 [16, 768, 2304], P('row', None, 'col'), may hold values from -0.3984375 to 0.3984375
- eps_occ: float32 [16], replicated, may hold values from -2 to -0.5
- eps_vir: float32 [768], replicated, may hold values from 0.2 to 3
- fock_vir: bfloat16 [768, 768], replicated, may hold values from -2 to 2, as said below
Outputs:
- updated: bfloat16 [16, 16, 768, 768], P('row', 'col')
Inputs may be any that keep to these rules, and one draw needn't show every extreme that they name: fock_vir is zero on its diagonal.
All inputs are finite; a program needn't handle non-finite values.
Results may differ from a plain program's by a relative error of at most 0.019.
Values may be sent and summed in bfloat16 or wider, within the bound.
A program may use at most 64 MiB of HBM per device.

v0:
```python
import jax
import jax.numpy as jnp
from jax import lax
from jax.sharding import Mesh
from jax.sharding import PartitionSpec as P

COL = ("col_0", "col_1")
ROW = ("row_0", "row_1", "row_2")


def gathered_by_axis(shard, axes, dim):
    filled = shard
    for number in range(len(axes) - 1, -1, -1):
        filled = lax.all_gather(filled, axes[number], axis=dim, tiled=True)
    return filled


def split_up(shard, dim, peers):
    shape = shard.shape
    tiles = shard.reshape(*shape[:dim], peers, shape[dim] // peers, *shape[dim + 1 :])
    return jnp.moveaxis(tiles, dim, 0)


def sent_and_summed(shard, axis, dim):
    peers = lax.axis_size(axis)
    tiles = lax.all_to_all(split_up(shard, dim, peers), axis, 0, 0, tiled=True)
    return jnp.sum(tiles.astype(jnp.float32), axis=0)


def sum_in_two_steps(shard, axes, dim):
    far, near = axes
    tiles = split_up(shard, dim, lax.axis_size(far))
    nearer = sent_and_summed(tiles, near, dim + 1)
    arrived = lax.all_to_all(
        nearer.astype(jnp.bfloat16), far, split_axis=0, concat_axis=0, tiled=True
    )
    return arrived.astype(jnp.float32).sum(axis=0)


def sent_to_all(shard, axis):
    copies = jnp.broadcast_to(shard, (lax.axis_size(axis), *shard.shape))
    return lax.all_to_all(copies, axis, split_axis=0, concat_axis=0, tiled=True)


def joined_along(tiles, dim):
    tiles = jnp.moveaxis(tiles, 0, dim)
    shape = tiles.shape
    return tiles.reshape(*shape[:dim], shape[dim] * shape[dim + 1], *shape[dim + 2 :])


def gather_axes(shard, axes, dim):
    far, near = axes
    initial = sent_to_all(shard, far)
    tiles = jnp.swapaxes(sent_to_all(initial, near), 0, 1)
    return joined_along(tiles.reshape(-1, *shard.shape), dim)


def local(amplitudes, ints, eps_occ, eps_vir, fock_vir):
    occ_row = amplitudes.shape[0]
    occ_col = amplitudes.shape[1]
    second_ids = lax.axis_index(COL) * occ_col + jnp.arange(occ_col, dtype=jnp.int32)
    first_ids = lax.axis_index(ROW) * occ_row + jnp.arange(occ_row, dtype=jnp.int32)
    picker = (second_ids[:, None] == first_ids[None, :]).astype(jnp.bfloat16)
    full_rows = gathered_by_axis(ints, COL, 2)
    own_part = jnp.einsum("ji,iaq->jaq", picker, full_rows, preferred_element_type=jnp.float32)
    cross_part = own_part + jnp.einsum(
        "kjcb,kcq->jbq", amplitudes, full_rows, preferred_element_type=jnp.float32
    )
    share = sum_in_two_steps(cross_part.astype(jnp.bfloat16), (("row_0", "row_1"), "row_2"), 2)
    dressed_share = share.astype(jnp.bfloat16)
    dressed = gather_axes(dressed_share, (("row_0", "row_1"), "row_2"), 2)
    numer = jnp.einsum("iaq,jbq->ijab", full_rows, dressed, preferred_element_type=jnp.float32)
    numer = numer + jnp.einsum(
        "ijac,cb->ijab", amplitudes, fock_vir, preferred_element_type=jnp.float32
    )
    eps_first = lax.dynamic_slice_in_dim(eps_occ, lax.axis_index(ROW) * occ_row, occ_row, 0)
    eps_second = lax.dynamic_slice_in_dim(eps_occ, lax.axis_index(COL) * occ_col, occ_col, 0)
    denom = (
        eps_vir[None, None, :, None]
        + eps_vir[None, None, None, :]
        - eps_first[:, None, None, None]
        - eps_second[None, :, None, None]
    )
    return (amplitudes.astype(jnp.float32) - numer / denom).astype(jnp.bfloat16)


def solution(mesh):
    torus = Mesh(mesh.devices.reshape(4, 2, 2, 4, 4), ("row_0", "row_1", "row_2", "col_0", "col_1"))
    placed = (P(ROW, COL, None, None), P(ROW, None, COL), P(), P(), P())
    return jax.shard_map(
        local, mesh=torus, in_specs=placed, out_specs=P(ROW, COL, None, None), check_vma=False
    )
```

profile of v0, /device:TPU:65, one launch (start us, length us, event | category | flops | bytes accessed | tf_op | source)
XLA Modules:
  0.0 227.9 jit_solution(11838358263147826158)
XLA Ops:
  6.5 0.0 copy-start
  6.5 0.0 all-gather.2.cloned.1.call-start
  6.5 18.4 %all_gather.6 = bf16[1,768,576]{1,2,0:T(8,128)(2,1)} all-gather(bf16[1,768,144]{1,2,0:T(8,128)(2,1)} %param.6), channel_id=1, replica_groups=mesh['row_0'=4,'row_1'=2,'row_2'=2,'col_0'=4,'col_1'=4] {'col_1'}, dimensions={2}, use_global_device_ids=true | all-gather | bytes 1105920 | tf_op jit(solution)/shard_map/all_gather | solution.py:14
  24.9 0.0 all-gather.2.cloned.1.call-update
  25.0 0.0 copy-start.2
  25.0 49.2 %all-gather.2.cloned.1.call-done = bf16[1,768,2304]{1,2,0:T(8,128)(2,1)} async-done(((bf16[1,768,576]{1,2,0:T(8,128)(2,1)}), bf16[1,768,2304]{1,2,0:T(8,128)(2,1)}) %all-gather.2.cloned.1.call-update) | async-done | bytes 3538960 | tf_op jit(solution)/shard_map/all_gather | solution.py:14
  74.1 5.8 %copy.16 = bf16[1,768,2304]{2,1,0:T(8,128)(2,1)} copy(bf16[1,768,2304]{1,2,0:T(8,128)(2,1)} %all-gather.2.cloned.1.call-done) | data formatting | bytes 7077888 | tf_op jit(solution)/shard_map/all_gather | solution.py:14
  79.9 0.0 copy-done.2
  79.9 7.1 %add_convert_fusion = bf16[768,2304]{1,0:T(8,128)(2,1)} fusion(bf16[1,768,2304]{1,2,0:T(8,128)(2,1)} %all-gather.2.cloned.1.call-done, bf16[1,768,2304]{2,1,0:T(8,128)(2,1)} %copy.16, f32[]{:T(128)S(6)} %convert.8, bf16[1,1,768,768]{3,2,1,0:T(8,128)(2,1)S(1)} %copy-done.2), kind=kOutput, calls=%fused_computation | convolution fusion | flops 2724986880 | bytes 11796484 | tf_op jit(solution)/shard_map/kjcb,kcq->jbq/dot_general | solution.py:66
  87.0 5.8 %copy.17 = bf16[768,2304]{0,1:T(8,128)(2,1)} copy(bf16[768,2304]{1,0:T(8,128)(2,1)} %add_convert_fusion) | data formatting | bytes 7077888 | tf_op jit(solution)/shard_map/convert_element_type | solution.py:69
  92.8 2.2 copy.18
  95.0 8.0 %all_to_all.23 = bf16[2,8,1,768,144]{3,4,1,2,0:T(8,128)(2,1)} all-to-all(bf16[2,8,1,768,144]{3,4,1,2,0:T(8,128)(2,1)S(1)} %copy.18), channel_id=1, replica_groups=mesh['row_0'=4,'row_1'=2,'row_2'=2,'col_0'=4,'col_1'=4] {'row_2'}, dimensions={0} | all-to-all | bytes 7077888 | tf_op jit(solution)/shard_map/all_to_all | solution.py:26
  103.0 4.4 %reduce_sum.26 = bf16[8,768,144]{1,2,0:T(8,128)(2,1)} reduce(bf16[2,8,1,768,144]{3,4,1,2,0:T(8,128)(2,1)} %all_to_all.23, bf16[]{:T(256)} %constant.30.clone.1), dimensions={0,2}, to_apply=%region_0.0 | reduce | flops 884736 | bytes 5308418 | tf_op jit(solution)/shard_map/reduce_sum | solution.py:27
  107.4 53.1 %all_to_all.24 = bf16[8,1,768,144]{2,3,1,0:T(8,128)(2,1)S(1)} all-to-all(bf16[8,1,768,144]{2,3,1,0:T(8,128)(2,1)} %bitcast.50), channel_id=1, replica_groups=mesh['row_0'=4,'row_1'=2,'row_2'=2,'col_0'=4,'col_1'=4] {'row_0','row_1'}, dimensions={0} | all-to-all | bytes 3538944 | tf_op jit(solution)/shard_map/all_to_all | solution.py:34
  160.5 0.3 reduce_sum.28
  160.8 1.3 broadcast_in_dim.4
  162.1 0.0 copy-start.4
  162.1 3.7 %all-to-all-start.2 = ((bf16[8,1,768,144]{2,3,1,0:T(8,128)(2,1)}), bf16[8,1,768,144]{2,3,1,0:T(8,128)(2,1)S(1)}, u32[]{:S(2)}, u32[]{:S(2)}) async-start(bf16[8,1,768,144]{2,3,1,0:T(8,128)(2,1)} %broadcast_in_dim.4), calls=%async_computation.2 | async-start | bytes 3538944 | tf_op jit(solution)/shard_map/all_to_all | solution.py:42
  165.9 2.4 %copy.15 = bf16[1,1,768,768]{2,3,0,1:T(8,128)(2,1)} copy(bf16[1,1,768,768]{3,2,1,0:T(8,128)(2,1)} %param.5) | data formatting | bytes 2359296 | tf_op args[0]
  168.2 0.0 copy-done.4
  168.2 0.7 fusion.11
  168.9 0.0 copy-done
  168.9 3.8 %fusion.8 = f32[768,768]{0,1:T(8,128)} fusion(bf16[768,768]{1,0:T(8,128)(2,1)S(1)} %copy-done, bf16[1,1,768,768]{3,2,1,0:T(8,128)(2,1)} %param.5), kind=kOutput, calls=%fused_computation.8 | convolution fusion | flops 905969664 | bytes 4718592 | tf_op jit(solution)/shard_map/ijac,cb->ijab/dot_general | solution.py:73
  172.7 32.0 %all-to-all-done.2 = bf16[8,1,768,144]{2,3,1,0:T(8,128)(2,1)S(1)} async-done(((bf16[8,1,768,144]{2,3,1,0:T(8,128)(2,1)}), bf16[8,1,768,144]{2,3,1,0:T(8,128)(2,1)S(1)}, u32[]{:S(2)}, u32[]{:S(2)}) %all-to-all-start.2) | async-done | bytes 1769504 | tf_op jit(solution)/shard_map/all_to_all | solution.py:42
  204.7 0.2 broadcast_in_dim.5
  205.0 6.8 %all_to_all.25 = bf16[2,8,1,768,144]{3,4,2,1,0:T(8,128)(2,1)S(1)} all-to-all(bf16[2,8,1,768,144]{3,4,2,1,0:T(8,128)(2,1)S(1)} %broadcast_in_dim.5), channel_id=1, replica_groups=mesh['row_0'=4,'row_1'=2,'row_2'=2,'col_0'=4,'col_1'=4] {'row_2'}, dimensions={0} | all-to-all | bytes 7077888 | tf_op jit(solution)/shard_map/all_to_all | solution.py:42
  211.8 0.0 copy-start.1
  211.8 0.0 copy-start.3
  211.8 0.0 copy-start.5
  211.8 0.0 copy-start.6
  211.8 0.2 copy.21
  212.0 1.8 copy-done.1
  213.8 0.3 copy-done.3
  214.1 0.0 copy-done.5
  214.1 0.8 copy-done.6
  214.9 4.7 %fusion.5 = bf16[1,1,768,768]{2,3,0,1:T(8,128)(2,1)S(1)} fusion(f32[768,768]{0,1:T(8,128)S(1)} %copy-done.6, bf16[1,1,768,768]{2,3,0,1:T(8,128)(2,1)S(1)} %copy-done.3, bf16[768,2304]{0,1:T(8,128)(2,1)S(1)} %bitcast.52, bf16[1,768,2304]{1,2,0:T(8,128)(2,1)S(1)} %copy-done.1, f32[]{:T(128)} %bitcast.17, f32[]{:T(128)} %bitcast.16, f32[768]{0:T(1024)S(1)} %copy-done.5), kind=kOutput, calls=%fused_computation.7 | convolution fusion | flops 2722627584 | bytes 11799560 | tf_op jit(solution)/shard_map/iaq,jbq->ijab/dot_general | solution.py:72
  219.6 1.5 copy.23
Async XLA Ops:
  6.5 162.4 %copy-start = (bf16[768,768]{1,0:T(8,128)(2,1)S(1)}, bf16[768,768]{1,0:T(8,128)(2,1)}, u32[]{:S(2)}) copy-start(bf16[768,768]{1,0:T(8,128)(2,1)} %param.9) | copy-start | bytes 3538948
  6.5 67.6 %all-gather.2.cloned.1.call-start = ((), (), s32[]{:S(2)}) async-start(), calls=%async_computation.4 | async-start | bytes 4423680 | tf_op jit(solution)/shard_map/all_gather | solution.py:14
  25.0 55.0 %copy-start.2 = (bf16[1,1,768,768]{3,2,1,0:T(8,128)(2,1)S(1)}, bf16[1,1,768,768]{3,2,1,0:T(8,128)(2,1)}, u32[]{:S(2)}) copy-start(bf16[1,1,768,768]{3,2,1,0:T(8,128)(2,1)} %param.5) | copy-start | bytes 3538948
  162.1 6.1 %copy-start.4 = (f32[16]{0:T(128)S(1)}, f32[16]{0:T(128)}, u32[]{:S(2)}) copy-start(f32[16]{0:T(128)} %param.7) | copy-start | bytes 196
  162.1 42.6 %all-to-all-start.2 = ((bf16[8,1,768,144]{2,3,1,0:T(8,128)(2,1)}), bf16[8,1,768,144]{2,3,1,0:T(8,128)(2,1)S(1)}, u32[]{:S(2)}, u32[]{:S(2)}) async-start(bf16[8,1,768,144]{2,3,1,0:T(8,128)(2,1)} %broadcast_in_dim.4), calls=%async_computation.2 | async-start | bytes 3538944 | tf_op jit(solution)/shard_map/all_to_all | solution.py:42
  211.8 2.0 copy-start.1
  211.8 2.3 %copy-start.3 = (bf16[1,1,768,768]{2,3,0,1:T(8,128)(2,1)S(1)}, bf16[1,1,768,768]{2,3,0,1:T(8,128)(2,1)}, u32[]{:S(2)}) copy-start(bf16[1,1,768,768]{2,3,0,1:T(8,128)(2,1)} %copy.15) | copy-start | bytes 3538948
  211.8 2.3 %copy-start.5 = (f32[768]{0:T(1024)S(1)}, f32[768]{0:T(1024)}, u32[]{:S(2)}) copy-start(f32[768]{0:T(1024)} %param.8) | copy-start | bytes 9220
  211.8 3.1 %copy-start.6 = (f32[768,768]{0,1:T(8,128)S(1)}, f32[768,768]{0,1:T(8,128)}, u32[]{:S(2)}) copy-start(f32[768,768]{0,1:T(8,128)} %fusion.8) | copy-start | bytes 7077892
Sparse Core Ops, SparseCore 0:
  25.1 49.0 all-gather.1
where the time goes:
time: 229 us; the launch traced here: 228 us
  blocking collectives  86.3 us (38%)
  waiting for transfers between devices  81.2 us (35%)
  local copies, waits for them, and re-layouts  23 us (10%)
  matrix products  15.6 us (7%)
  between operations  13.5 us (6%)
  other arithmetic  4.7 us (2%)
  starting transfers between devices  3.72 us (2%)
    all_to_all x1, blocking collectives, sum_in_two_steps(): lax.all_to_all(nearer.astype(jnp.bfloat16), far, split_axis=0, concat_axi...  53.1 us
    all_gather x1, waiting for transfers between devices, gathered_by_axis(): filled = lax.all_gather(filled, axes[number], axis=dim, tiled=True)  49.2 us
    all_to_all x1, waiting for transfers between devices, sent_to_all(): return lax.all_to_all(copies, axis, split_axis=0, concat_axis=0, tiled=True)  32 us
    all_gather x1, blocking collectives, gathered_by_axis(): filled = lax.all_gather(filled, axes[number], axis=dim, tiled=True)  18.4 us
    all_to_all x1, blocking collectives, sent_and_summed(): tiles = lax.all_to_all(split_up(shard, dim, peers), axis, 0, 0, tiled=True)  8.04 us
    dot_general x1, matrix products, local(): jnp.einsum('kjcb,kcq->jbq', amplitudes, full_rows, preferred_element_type...  7.06 us
    all_to_all x1, blocking collectives, sent_to_all(): return lax.all_to_all(copies, axis, split_axis=0, concat_axis=0, tiled=True)  6.82 us
    all_gather x1, local copies, waits for them, and re-layouts, gathered_by_axis(): filled = lax.all_gather(filled, axes[number], axis=dim, tiled=True)  5.81 us
  transfers between devices with their start and end apart: 2, of which 2 were waited for; matrix products, arithmetic and copies ran while one was open for 3% of the time, Pallas kernels for 0%

commit v1 on v0

v1 whole, which is shorter than its diff:
```python
import functools

import jax
import jax.numpy as jnp
from jax import lax
from jax.experimental import pallas as pl
from jax.experimental.pallas import tpu as pltpu
from jax.sharding import Mesh
from jax.sharding import PartitionSpec as P

COL = ("y", "zl")
ROW = ("x", "zh", "core")
STAGES = 4
MESH = pl.DeviceIdType.MESH
BF = jnp.bfloat16
F32 = jnp.float32


def kernel(
    ints, amp, fock, eps_occ, eps_vir, out,
    gath, ampv, fockv, acc, rden,
    give, take, part, x1s, x1r, x2s, x2r, zs, zr, dres,
    stage_out,
    in_sem, out_sem, send_sem, ra, rcore, rx1, rx2, rz, rd,
):
    depth = ints.shape[0]
    vir = ints.shape[1]
    half = vir // 2
    cut = (depth // 2 + 15) // 16 * 16
    x, zh, p = lax.axis_index("x"), lax.axis_index("zh"), lax.axis_index("core")
    y, zl = lax.axis_index("y"), lax.axis_index("zl")
    side = zl // 2
    m = zl + side * (3 - 2 * zl)
    dz = 1 - 2 * side
    rows = [m, 1 - m, 2, 3]
    rows = [v + side * (3 - 2 * v) for v in rows]
    yu, yd, yo = lax.rem(y + 1, 4), lax.rem(y + 3, 4), lax.rem(y + 2, 4)
    xu, xd, xo = lax.rem(x + 1, 4), lax.rem(x + 3, 4), lax.rem(x + 2, 4)
    me = dict(x=x, zh=zh, core=p, y=y, zl=zl)

    def at(**where):
        there = {**me, **where}
        return tuple(there[name] for name in ("x", "zh", "core", "y", "zl"))

    z_plus, z_minus = at(zl=zl + dz), at(zl=zl - dz)
    y_up, y_down = at(y=yu), at(y=yd)
    x_up, x_down = at(x=xu), at(x=xd)
    z_far, mate = at(zh=1 - zh), at(core=1 - p)

    started = []

    def send(src, dst, sem, where):
        copy = pltpu.make_async_remote_copy(
            src_ref=src, dst_ref=dst, send_sem=send_sem.at[len(started)],
            recv_sem=sem, device_id=where, device_id_type=MESH,
        )
        copy.start()
        started.append((copy, None))

    def send_if_inner(src, dst, sem, where):
        copy = pltpu.make_async_remote_copy(
            src_ref=src, dst_ref=dst, send_sem=send_sem.at[len(started)],
            recv_sem=sem, device_id=where, device_id_type=MESH,
        )

        @pl.when(m == 1)
        def _():
            copy.start()

        started.append((copy, m == 1))

    def arrived(dst, sem):
        pltpu.make_async_remote_copy(
            src_ref=dst, dst_ref=dst, send_sem=send_sem.at[0],
            recv_sem=sem, device_id=mate, device_id_type=MESH,
        ).wait_recv()

    own = pltpu.make_async_copy(ints, gath.at[rows[0], y], in_sem.at[0])
    own.start()
    loads = [
        pltpu.make_async_copy(amp.at[:, pl.ds(0, half)], ampv.at[0], in_sem.at[1]),
        pltpu.make_async_copy(amp.at[:, pl.ds(half, half)], ampv.at[1], in_sem.at[2]),
        pltpu.make_async_copy(fock, fockv, in_sem.at[3]),
    ]
    for load in loads:
        load.start()

    barrier = pltpu.get_barrier_semaphore()
    for where in (z_plus, y_up, y_down, x_up, x_down, z_far, mate):
        pl.semaphore_signal(barrier, inc=1, device_id=where, device_id_type=MESH)

    @pl.when(m == 1)
    def _():
        pl.semaphore_signal(barrier, inc=1, device_id=z_minus, device_id_type=MESH)

    own.wait()
    pl.semaphore_wait(barrier, 7 + m)

    lo, hi = pl.ds(0, half), pl.ds(half, half)

    def block(k, q):
        return gath.at[rows[k], q]

    def send_y(k):
        b = block(k, y)
        s = ra.at[rows[k], y]
        send(b.at[:, lo], b.at[:, lo], s.at[0], y_up)
        send(b.at[:, hi], b.at[:, hi], s.at[1], y_down)
        send(b.at[:, hi], b.at[:, hi], s.at[1], y_up)
        send(b.at[:, lo], b.at[:, lo], s.at[0], y_down)

    def start_own():
        b, s = block(0, y), ra.at[rows[0], y, 2]
        send(b, b, s, z_plus)
        send_if_inner(b, b, s, z_minus)
        send_y(0)

    def z_arrive(k):
        b, s = block(k, y), ra.at[rows[k], y, 2]
        arrived(b, s)
        send_if_inner(b, b, s, z_plus if k == 1 else z_minus)

    def y_first(k):
        b, s = block(k, yd), ra.at[rows[k], yd, 0]
        arrived(b.at[:, lo], s)
        send(b.at[:, lo], b.at[:, lo], s, y_up)
        b, s = block(k, yu), ra.at[rows[k], yu, 1]
        arrived(b.at[:, hi], s)
        send(b.at[:, hi], b.at[:, hi], s, y_down)

    def y_second(k):
        b, s = block(k, yd), ra.at[rows[k], yd, 1]
        arrived(b.at[:, hi], s)
        b, s = block(k, yu), ra.at[rows[k], yu, 0]
        arrived(b.at[:, lo], s)

    def y_opposite(k):
        b, s = block(k, yo), ra.at[rows[k], yo]
        arrived(b.at[:, lo], s.at[0])
        arrived(b.at[:, hi], s.at[1])

    mine_term = (x * 4 + zh * 2 + p == y * 4 + zl).astype(jnp.int32).astype(F32)

    def cross(k, q):
        b = block(k, q)

        def columns(h):
            got = jnp.dot(b[...], ampv[h], preferred_element_type=F32)
            return got

        def own_columns(h):
            return jnp.where(h == 0, b[:, :half], b[:, half:]).astype(F32) * mine_term

        give[k, q] = (columns(1 - p) + own_columns(1 - p)).astype(BF)
        send(give.at[k, q], take.at[k, q], rcore.at[k, q], mate)
        part[k, q] = columns(p) + own_columns(p)

    def merge_core(k):
        for q in (yo, yd, yu, y):
            arrived(take.at[k, q], rcore.at[k, q])
        x1s[k] = (part[k, xo] + take[k, xo].astype(F32)).astype(BF)
        send(x1s.at[k, pl.ds(0, cut)], x1r.at[k, pl.ds(0, cut)], rx1.at[k, 0], x_up)
        send(
            x1s.at[k, pl.ds(cut, depth - cut)], x1r.at[k, pl.ds(cut, depth - cut)],
            rx1.at[k, 1], x_down,
        )
        for q in (xu, xd, x):
            part[k, q] += take[k, q].astype(F32)

    def x_relay(k):
        head, tail = pl.ds(0, cut), pl.ds(cut, depth - cut)
        arrived(x1r.at[k, head], rx1.at[k, 0])
        x2s[k, 0, :cut] = (part[k, xu, :cut] + x1r[k, :cut].astype(F32)).astype(BF)
        x2s[k, 0, cut:] = part[k, xu, cut:].astype(BF)
        send(x2s.at[k, 0], x2r.at[k, 0], rx2.at[k, 0], x_up)
        arrived(x1r.at[k, tail], rx1.at[k, 1])
        x2s[k, 1, :cut] = part[k, xd, :cut].astype(BF)
        x2s[k, 1, cut:] = (part[k, xd, cut:] + x1r[k, cut:].astype(F32)).astype(BF)
        send(x2s.at[k, 1], x2r.at[k, 1], rx2.at[k, 1], x_down)

    def x_done(k):
        arrived(x2r.at[k, 0], rx2.at[k, 0])
        arrived(x2r.at[k, 1], rx2.at[k, 1])
        zs[k] = (part[k, x] + (x2r[k, 0].astype(F32) + x2r[k, 1].astype(F32))).astype(BF)
        send(zs.at[k], zr.at[k], rz.at[k], z_far)

    def z_done(k):
        arrived(zr.at[k], rz.at[k])
        dres[k, p, x] = (zs[k].astype(F32) + zr[k].astype(F32)).astype(BF)
        b, s = dres.at[k, p, x], rd.at[k, p, x]
        send(b, b, s.at[0], x_up)
        send(b, b, s.at[0], x_down)
        send(b, b, s.at[0], mate)

    def spread(k):
        head, tail = pl.ds(0, cut), pl.ds(cut, depth - cut)
        b, s = dres.at[k, p, xd], rd.at[k, p, xd]
        arrived(b, s.at[0])
        send(b.at[head], b.at[head], s.at[0], x_up)
        send(b, b, s.at[0], mate)
        b, s = dres.at[k, p, xu], rd.at[k, p, xu]
        arrived(b, s.at[0])
        send(b.at[tail], b.at[tail], s.at[1], x_down)
        send(b, b, s.at[0], mate)

    def spread_far(k):
        head, tail = pl.ds(0, cut), pl.ds(cut, depth - cut)
        b, s = dres.at[k, p, xo], rd.at[k, p, xo]
        arrived(b.at[head], s.at[0])
        arrived(b.at[tail], s.at[1])
        send(b, b, s.at[0], mate)

    def contract(k):
        for q in (x, xd, xu, xo):
            arrived(dres.at[k, 1 - p, q], rd.at[k, 1 - p, q, 0])
        left = gath[rows[k]].reshape(4 * depth, vir)

        @pl.loop(0, 2)
        def _(h):
            right = dres[k, h].reshape(4 * depth, half)
            acc[h] += lax.dot_general(
                left, right, (((0,), (0,)), ((), ())), preferred_element_type=F32
            )

    def early():
        for load in loads:
            load.wait()
        level = eps_occ[x * 4 + zh * 2 + p]
        level2 = eps_occ[y * 4 + zl]
        across = eps_vir[...]
        down = jnp.broadcast_to(across, (128, vir)).T[:, :1]
        for h in range(2):
            f = fockv[:, h * half : (h + 1) * half]
            acc[h] = jnp.dot(ampv[0], f[:half], preferred_element_type=F32) + jnp.dot(
                ampv[1], f[half:], preferred_element_type=F32
            )
            row = across[:, h * half : (h + 1) * half]
            rden[h] = 1.0 / (((down + row) - level) - level2)

    steps = [(0.0, start_own, ()), (0.1, early, ()), (1.0, cross, (0, y))]
    for k in range(STAGES):
        base = 8.1 * k
        if k:
            steps.append((5.4 * k + 1.5, z_arrive, (k,)))
            steps.append((max(5.4 * k + 1.6, 4.3 + 8.1 * (k - 1) + 0.1), send_y, (k,)))
            steps.append((max(5.4 * k + 1.7, 4.3 + 8.1 * (k - 1) + 0.2), cross, (k, y)))
        steps.append((base + 4.3, y_first, (k,)))
        steps.append((base + 7.0, y_second, (k,)))
        steps.append((base + 7.1, cross, (k, yd)))
        steps.append((base + 7.2, cross, (k, yu)))
        done = base + 9.6
        steps.append((done, y_opposite, (k,)))
        steps.append((done + 0.1, cross, (k, yo)))
        steps.append((done + 3.0, merge_core, (k,)))
        steps.append((done + 6.0, x_relay, (k,)))
        steps.append((done + 10.0, x_done, (k,)))
        steps.append((done + 18.0, z_done, (k,)))
        steps.append((done + 22.0, spread, (k,)))
        steps.append((done + 24.0, spread_far, (k,)))
        steps.append((done + 27.0, contract, (k,)))
    for _, step, which in sorted(steps, key=lambda s: s[0]):
        step(*which)

    for h in range(2):
        stage_out[:, h * half : (h + 1) * half] = (
            ampv[h].astype(F32) - acc[h] * rden[h]
        ).astype(BF)
    back = pltpu.make_async_copy(stage_out, out, out_sem)
    back.start()
    for copy, guard in started:
        if guard is None:
            copy.wait_send()
        else:
            pl.when(guard)(copy.wait_send)
    back.wait()


def local(amplitudes, ints, eps_occ, eps_vir, fock_vir):
    vir, depth = ints.shape[1], ints.shape[2]
    half = vir // 2
    anywhere = pl.BlockSpec(memory_space=pl.ANY)
    dma = pltpu.SemaphoreType.DMA
    updated = pl.pallas_call(
        kernel,
        out_shape=jax.ShapeDtypeStruct((vir, vir), BF),
        in_specs=[
            anywhere, anywhere, anywhere,
            pl.BlockSpec(memory_space=pltpu.SMEM),
            pl.BlockSpec(memory_space=pltpu.VMEM),
        ],
        out_specs=anywhere,
        scratch_shapes=[
            pltpu.VMEM((4, 4, depth, vir), BF),
            pltpu.VMEM((2, vir, half), BF),
            pltpu.VMEM((vir, vir), BF),
            pltpu.VMEM((2, vir, half), F32),
            pltpu.VMEM((2, vir, half), F32),
            pltpu.VMEM((STAGES, 4, depth, half), BF),
            pltpu.VMEM((STAGES, 4, depth, half), BF),
            pltpu.VMEM((STAGES, 4, depth, half), F32),
            pltpu.VMEM((STAGES, depth, half), BF),
            pltpu.VMEM((STAGES, depth, half), BF),
            pltpu.VMEM((STAGES, 2, depth, half), BF),
            pltpu.VMEM((STAGES, 2, depth, half), BF),
            pltpu.VMEM((STAGES, depth, half), BF),
            pltpu.VMEM((STAGES, depth, half), BF),
            pltpu.VMEM((STAGES, 2, 4, depth, half), BF),
            pltpu.VMEM((vir, vir), BF),
            dma((4,)), dma, dma((128,)),
            dma((4, 4, 3)), dma((STAGES, 4)), dma((STAGES, 2)), dma((STAGES, 2)),
            dma((STAGES,)), dma((STAGES, 2, 4, 2)),
        ],
        compiler_params=pltpu.CompilerParams(
            collective_id=0, has_side_effects=True, vmem_limit_bytes=60 * 1024 * 1024
        ),
        name="doubles_update",
    )(ints[0].T, amplitudes[0, 0], fock_vir, eps_occ, eps_vir[None, :])
    return updated[None, None]


def solution(mesh):
    torus = Mesh(mesh.devices.reshape(4, 2, 2, 4, 4), ("x", "zh", "core", "y", "zl"))
    placed = (P(ROW, COL, None, None), P(ROW, None, COL), P(), P(), P())
    return jax.shard_map(
        local, mesh=torus, in_specs=placed, out_specs=P(ROW, COL, None, None), check_vma=False
    )
```

time: 229 us -> 90.6 us (0.40)
  the two profiles are of different devices: /device:TPU:65 before, /device:TPU:1 now
where the time goes in v1:
time: 90.6 us; the launch traced here: 90.4 us
  Pallas kernels  86.8 us (96%)
  local copies, waits for them, and re-layouts  3.63 us (4%)
    pallas_call x1, Pallas kernels, local(): pl.pallas_call(kernel, out_shape=jax.ShapeDtypeStruct((vir, vir), BF), in...  86.8 us
    unnamed x1, local copies, waits for them, and re-layouts  2.36 us

profile of v1, /device:TPU:1, one launch (start us, length us, event | category | flops | bytes accessed | tf_op | source)
XLA Modules:
  0.0 90.4 jit_solution(11373494337825660718)
XLA Ops:
  0.0 1.3 %broadcast_in_dim.6.eps_vir = f32[1,768]{1,0:T(1,128)} reshape(f32[768]{0:T(1024)} %param.8) | data formatting | bytes 6144 | tf_op jit(solution)/shard_map/broadcast_in_dim | solution.py:317
  1.3 86.8 %doubles_update.1 = bf16[768,768]{1,0:T(8,128)(2,1)} custom-call(bf16[144,768]{1,0:T(8,128)(2,1)} %bitcast.7, bf16[768,768]{1,0:T(8,128)(2,1)} %bitcast.6, bf16[768,768]{1,0:T(8,128)(2,1)} %fock.1, f32[16]{0:T(128)} %eps_occ.1, f32[1,768]{1,0:T(1,128)} %broadcast_in_dim.6.eps_vir), custom_call_target="tpu_custom_call" | custom-call | tf_op jit(solution)/shard_map/doubles_update/pallas_call | solution.py:283
  88.0 2.4 %copy.7 = bf16[1,1,768,768]{3,2,1,0:T(8,128)(2,1)} copy(bf16[1,1,768,768]{3,2,1,0:T(8,128)(2,1)} %bitcast.5) | data formatting | bytes 2359296

commit v2 on v0

v2 whole, which is shorter than its diff:
```python
import jax
import jax.numpy as jnp
from jax import lax
from jax.experimental import pallas as pl
from jax.experimental.pallas import tpu as pltpu
from jax.sharding import Mesh
from jax.sharding import PartitionSpec as P

COL = ("y", "zl")
ROW = ("x", "zh", "core")
MESH = pl.DeviceIdType.MESH
BF = jnp.bfloat16
F32 = jnp.float32

CHUNKS = (
    (0, 0, 144), (1, 0, 144), (2, 0, 144), (3, 0, 64), (3, 64, 144),
)
ORDER = (
    ("start_own", 0, 0), ("load_wait", 0, 0), ("cross", 0, "y"), ("fock", 0, 0), ("y_first", 0, 0),
    ("z_forward", 1, 0), ("z_forward", 2, 0), ("z_arrive", 1, 0), ("send_y", 1, 0), ("y_second", 0, 0),
    ("cross", 0, "d"), ("cross", 0, "u"), ("cross", 1, "y"), ("y_opposite", 0, 0), ("cross", 0, "o"),
    ("y_first", 1, 0), ("merge_core", 0, 0), ("z_forward", 3, 0), ("z_arrive", 2, 0), ("send_y", 2, 0),
    ("cross", 2, "y"), ("y_second", 1, 0), ("cross", 1, "d"), ("cross", 1, "u"), ("x_relay", 0, 0),
    ("y_opposite", 1, 0), ("cross", 1, "o"), ("y_first", 2, 0), ("z_arrive", 3, 0), ("send_y", 3, 0),
    ("cross", 3, "y"), ("merge_core", 1, 0), ("x_done", 0, 0), ("cross", 4, "y"), ("y_second", 2, 0),
    ("cross", 2, "d"), ("cross", 2, "u"), ("x_relay", 1, 0), ("y_opposite", 2, 0), ("cross", 2, "o"),
    ("y_first", 3, 0), ("send_y", 4, 0), ("y_second", 3, 0), ("cross", 3, "d"), ("cross", 3, "u"),
    ("merge_core", 2, 0), ("x_done", 1, 0), ("y_opposite", 3, 0), ("cross", 3, "o"), ("y_first", 4, 0),
    ("x_relay", 2, 0), ("merge_core", 3, 0), ("y_second", 4, 0), ("cross", 4, "d"), ("cross", 4, "u"),
    ("y_opposite", 4, 0), ("cross", 4, "o"), ("z_done", 0, 0), ("x_done", 2, 0), ("merge_core", 4, 0),
    ("x_relay", 3, 0), ("spread", 0, 0), ("x_relay", 4, 0), ("x_done", 3, 0), ("z_done", 1, 0),
    ("spread_far", 0, 0), ("x_done", 4, 0), ("contract", 0, 0), ("spread", 1, 0), ("z_done", 2, 0),
    ("spread_far", 1, 0), ("z_done", 3, 0), ("contract", 1, 0), ("spread", 2, 0), ("spread", 3, 0),
    ("z_done", 4, 0), ("spread_far", 2, 0), ("spread_far", 3, 0), ("spread", 4, 0), ("contract", 2, 0),
    ("contract", 3, 0), ("spread_far", 4, 0), ("contract", 4, 0),
)


def kernel(
    ints, amp, fock, out,
    gath, ampv, fockv, acc, temp,
    give, take, part, x1s, x1r, x2s, x2r, zs, zr, dres,
    in_sem, out_sem, send_sem, ra, raz, rcore, rx1, rx2, rz, rd,
):
    vir = ints.shape[1]
    half = vir // 2
    x, zh, p = lax.axis_index("x"), lax.axis_index("zh"), lax.axis_index("core")
    y, zl = lax.axis_index("y"), lax.axis_index("zl")
    side = zl // 2
    m = zl + side * (3 - 2 * zl)
    dz = 1 - 2 * side
    rows = [v + side * (3 - 2 * v) for v in (m, 1 - m, 2, 3)]
    yu, yd, yo = lax.rem(y + 1, 4), lax.rem(y + 3, 4), lax.rem(y + 2, 4)
    xu, xd, xo = lax.rem(x + 1, 4), lax.rem(x + 3, 4), lax.rem(x + 2, 4)
    of_y = {"y": y, "u": yu, "d": yd, "o": yo}
    me = dict(x=x, zh=zh, core=p, y=y, zl=zl)

    def at(**where):
        there = {**me, **where}
        return tuple(there[name] for name in ("x", "zh", "core", "y", "zl"))

    z_plus, z_minus = at(zl=zl + dz), at(zl=zl - dz)
    y_up, y_down = at(y=yu), at(y=yd)
    x_up, x_down = at(x=xu), at(x=xd)
    z_far, mate = at(zh=1 - zh), at(core=1 - p)

    started = []

    def send(src, dst, sem, where, guard=None):
        copy = pltpu.make_async_remote_copy(
            src_ref=src, dst_ref=dst, send_sem=send_sem.at[len(started)],
            recv_sem=sem, device_id=where, device_id_type=MESH,
        )
        if guard is None:
            copy.start()
        else:
            pl.when(guard)(copy.start)
        started.append((copy, guard))

    def arrived(dst, sem):
        pltpu.make_async_remote_copy(
            src_ref=dst, dst_ref=dst, send_sem=send_sem.at[0],
            recv_sem=sem, device_id=mate, device_id_type=MESH,
        ).wait_recv()

    own = pltpu.make_async_copy(ints, gath.at[rows[0], y], in_sem.at[0])
    own.start()
    loads = [
        pltpu.make_async_copy(amp.at[:, pl.ds(0, half)], ampv.at[0], in_sem.at[1]),
        pltpu.make_async_copy(amp.at[:, pl.ds(half, half)], ampv.at[1], in_sem.at[2]),
        pltpu.make_async_copy(fock, fockv, in_sem.at[3]),
    ]
    for load in loads:
        load.start()

    barrier = pltpu.get_barrier_semaphore()
    for where in (z_plus, y_up, y_down, x_up, x_down, z_far, mate):
        pl.semaphore_signal(barrier, inc=1, device_id=where, device_id_type=MESH)

    @pl.when(m == 1)
    def _():
        pl.semaphore_signal(barrier, inc=1, device_id=z_minus, device_id_type=MESH)

    own.wait()
    pl.semaphore_wait(barrier, 7 + m)

    lo, hi = pl.ds(0, half), pl.ds(half, half)
    is_mine = x * 4 + zh * 2 + p == y * 4 + zl

    def span(i):
        return CHUNKS[i][1], CHUNKS[i][2]

    def cut(i):
        a, b = span(i)
        middle = a + ((b - a) // 16 + i % 2) // 2 * 16
        return pl.ds(a, middle - a), pl.ds(middle, b - middle)

    def whole(i):
        a, b = span(i)
        return pl.ds(a, b - a)

    def block(i, q):
        return gath.at[rows[CHUNKS[i][0]], q, whole(i)]

    def send_y(i):
        b, s = block(i, y), ra.at[i, y]
        send(b.at[:, lo], b.at[:, lo], s.at[0], y_up)
        send(b.at[:, hi], b.at[:, hi], s.at[1], y_down)
        send(b.at[:, hi], b.at[:, hi], s.at[1], y_up)
        send(b.at[:, lo], b.at[:, lo], s.at[0], y_down)

    def start_own():
        b, s = gath.at[rows[0], y], raz.at[rows[0]]
        send(b, b, s, z_plus)
        send(b, b, s, z_minus, m == 1)
        for i, chunk in enumerate(CHUNKS):
            if chunk[0] == 0:
                send_y(i)

    def z_forward(k):
        b, s = gath.at[rows[k], y], raz.at[rows[k]]
        pl.when(m == 1)(lambda: arrived(b, s))
        send(b, b, s, z_plus if k == 1 else z_minus, m == 1)

    def z_arrive(k):
        b, s = gath.at[rows[k], y], raz.at[rows[k]]
        pl.when(m == 0)(lambda: arrived(b, s))

    def y_first(i):
        b, s = block(i, yd), ra.at[i, yd, 0]
        arrived(b.at[:, lo], s)
        send(b.at[:, lo], b.at[:, lo], s, y_up)
        b, s = block(i, yu), ra.at[i, yu, 1]
        arrived(b.at[:, hi], s)
        send(b.at[:, hi], b.at[:, hi], s, y_down)

    def y_second(i):
        arrived(block(i, yd).at[:, hi], ra.at[i, yd, 1])
        arrived(block(i, yu).at[:, lo], ra.at[i, yu, 0])

    def y_opposite(i):
        arrived(block(i, yo).at[:, lo], ra.at[i, yo, 0])
        arrived(block(i, yo).at[:, hi], ra.at[i, yo, 1])

    def cross(i, which):
        k, (a, b), q = CHUNKS[i][0], span(i), of_y[which]
        left = gath.at[rows[k], q, whole(i)]

        def term(into, h):
            into[...] = jnp.dot(left[...], ampv[h], preferred_element_type=F32)
            for side_of in range(2):

                @pl.when(is_mine & (h == side_of))
                def _(side_of=side_of):
                    into[...] += left[:, side_of * half : (side_of + 1) * half].astype(F32)

        term(temp.at[pl.ds(0, b - a)], 1 - p)
        give[k, q, a:b] = temp[: b - a].astype(BF)
        sent = (k, q, whole(i))
        send(give.at[sent], take.at[sent], rcore.at[i, q], mate)
        term(part.at[k, q, whole(i)], p)

    def merge_core(i):
        k, (a, b) = CHUNKS[i][0], span(i)
        for q in (y, yd, yu, yo):
            arrived(take.at[k, q, whole(i)], rcore.at[i, q])
        x1s[k, a:b] = (part[k, xo, a:b] + take[k, xo, a:b].astype(F32)).astype(BF)
        head, tail = cut(i)
        send(x1s.at[k, head], x1r.at[k, head], rx1.at[i, 0], x_up)
        send(x1s.at[k, tail], x1r.at[k, tail], rx1.at[i, 1], x_down)
        for q in (xu, xd, x):
            part[k, q, a:b] += take[k, q, a:b].astype(F32)

    def x_relay(i):
        k, (a, b) = CHUNKS[i][0], span(i)
        head, tail = cut(i)
        arrived(x1r.at[k, head], rx1.at[i, 0])
        x2s[k, 0, head] = (part[k, xu, head] + x1r[k, head].astype(F32)).astype(BF)
        x2s[k, 0, tail] = part[k, xu, tail].astype(BF)
        send(x2s.at[k, 0, whole(i)], x2r.at[k, 0, whole(i)], rx2.at[i, 0], x_up)
        arrived(x1r.at[k, tail], rx1.at[i, 1])
        x2s[k, 1, head] = part[k, xd, head].astype(BF)
        x2s[k, 1, tail] = (part[k, xd, tail] + x1r[k, tail].astype(F32)).astype(BF)
        send(x2s.at[k, 1, whole(i)], x2r.at[k, 1, whole(i)], rx2.at[i, 1], x_down)

    def x_done(i):
        k, (a, b) = CHUNKS[i][0], span(i)
        arrived(x2r.at[k, 0, whole(i)], rx2.at[i, 0])
        arrived(x2r.at[k, 1, whole(i)], rx2.at[i, 1])
        both = x2r[k, 0, a:b].astype(F32) + x2r[k, 1, a:b].astype(F32)
        zs[k, a:b] = (part[k, x, a:b] + both).astype(BF)
        send(zs.at[k, whole(i)], zr.at[k, whole(i)], rz.at[i], z_far)

    def z_done(i):
        k, (a, b) = CHUNKS[i][0], span(i)
        arrived(zr.at[k, whole(i)], rz.at[i])
        dres[k, p, x, a:b] = (zs[k, a:b].astype(F32) + zr[k, a:b].astype(F32)).astype(BF)
        b, s = dres.at[k, p, x, whole(i)], rd.at[i, p, x]
        send(b, b, s.at[0], x_up)
        send(b, b, s.at[0], x_down)
        send(b, b, s.at[0], mate)

    def spread(i):
        k = CHUNKS[i][0]
        head, tail = cut(i)
        for q, piece, sem, where in ((xd, head, 0, x_up), (xu, tail, 1, x_down)):
            b, s = dres.at[k, p, q, whole(i)], rd.at[i, p, q]
            arrived(b, s.at[0])
            c = dres.at[k, p, q, piece]
            send(c, c, s.at[sem], where)
            send(b, b, s.at[0], mate)

    def spread_far(i):
        k = CHUNKS[i][0]
        head, tail = cut(i)
        arrived(dres.at[k, p, xo, head], rd.at[i, p, xo, 0])
        arrived(dres.at[k, p, xo, tail], rd.at[i, p, xo, 1])
        b = dres.at[k, p, xo, whole(i)]
        send(b, b, rd.at[i, p, xo, 0], mate)

    def put(h):
        return pltpu.make_async_copy(
            acc.at[pl.ds(h * half, half)], out.at[pl.ds(h * half, half)], out_sem.at[h]
        )

    def contract(i):
        k, (a, b) = CHUNKS[i][0], span(i)
        for q in (x, xd, xu, xo):
            arrived(dres.at[k, 1 - p, q, whole(i)], rd.at[i, 1 - p, q, 0])
        left = gath[rows[k], :, a:b].reshape(4 * (b - a), vir)
        right = jnp.concatenate(
            [dres[k, h, :, a:b].reshape(4 * (b - a), half) for h in range(2)], axis=-1
        )
        last = ORDER[-1] == ("contract", i, 0)
        for h in range(2):
            r = slice(h * half, (h + 1) * half)
            acc[r] += lax.dot_general(
                left[:, r], right, (((0,), (0,)), ((), ())), preferred_element_type=F32
            )
            if last:
                put(h).start()

    def load_wait():
        for load in loads:
            load.wait()

    def fock_term():
        acc[...] = jnp.dot(ampv[0], fockv[:half], preferred_element_type=F32) + jnp.dot(
            ampv[1], fockv[half:], preferred_element_type=F32
        )

    for name, i, which in ORDER:
        if name == "cross":
            cross(i, which)
        elif name == "start_own":
            start_own()
        elif name == "load_wait":
            load_wait()
        elif name == "fock":
            fock_term()
        else:
            {
                "z_arrive": z_arrive, "z_forward": z_forward, "send_y": send_y, "y_first": y_first,
                "y_second": y_second, "y_opposite": y_opposite, "merge_core": merge_core,
                "x_relay": x_relay, "x_done": x_done, "z_done": z_done, "spread": spread,
                "spread_far": spread_far, "contract": contract,
            }[name](i)

    for copy, guard in started:
        if guard is None:
            copy.wait_send()
        else:
            pl.when(guard)(copy.wait_send)
    for h in range(2):
        put(h).wait()


def local(amplitudes, ints, eps_occ, eps_vir, fock_vir):
    vir, depth = ints.shape[1], ints.shape[2]
    half = vir // 2
    n = len(CHUNKS)
    anywhere = pl.BlockSpec(memory_space=pl.ANY)
    dma = pltpu.SemaphoreType.DMA
    numer = pl.pallas_call(
        kernel,
        out_shape=jax.ShapeDtypeStruct((vir, vir), F32),
        in_specs=[anywhere] * 3,
        out_specs=anywhere,
        scratch_shapes=[
            pltpu.VMEM((4, 4, depth, vir), BF),
            pltpu.VMEM((2, vir, half), BF),
            pltpu.VMEM((vir, vir), BF),
            pltpu.VMEM((vir, vir), F32),
            pltpu.VMEM((depth, half), F32),
            pltpu.VMEM((4, 4, depth, half), BF),
            pltpu.VMEM((4, 4, depth, half), BF),
            pltpu.VMEM((4, 4, depth, half), F32),
            pltpu.VMEM((4, depth, half), BF),
            pltpu.VMEM((4, depth, half), BF),
            pltpu.VMEM((4, 2, depth, half), BF),
            pltpu.VMEM((4, 2, depth, half), BF),
            pltpu.VMEM((4, depth, half), BF),
            pltpu.VMEM((4, depth, half), BF),
            pltpu.VMEM((4, 2, 4, depth, half), BF),
            dma((4,)), dma((2,)), dma((5 + 23 * n,)),
            dma((n, 4, 2)), dma((4,)), dma((n, 4)), dma((n, 2)), dma((n, 2)),
            dma((n,)), dma((n, 2, 4, 2)),
        ],
        compiler_params=pltpu.CompilerParams(
            collective_id=0, has_side_effects=True, vmem_limit_bytes=60 * 1024 * 1024
        ),
        name="doubles_numerator",
    )(ints[0].T, amplitudes[0, 0], fock_vir)
    level = eps_occ[lax.axis_index(ROW)]
    level2 = eps_occ[lax.axis_index(COL)]
    denom = eps_vir[:, None] + eps_vir[None, :] - level - level2
    updated = (amplitudes[0, 0].astype(F32) - numer / denom).astype(BF)
    return updated[None, None]


def solution(mesh):
    torus = Mesh(mesh.devices.reshape(4, 2, 2, 4, 4), ("x", "zh", "core", "y", "zl"))
    placed = (P(ROW, COL, None, None), P(ROW, None, COL), P(), P(), P())
    return jax.shard_map(
        local, mesh=torus, in_specs=placed, out_specs=P(ROW, COL, None, None), check_vma=False
    )
```

time: 229 us -> 83.2 us (0.36)
  the two profiles are of different devices: /device:TPU:65 before, /device:TPU:1 now
where the time goes in v2:
time: 83.2 us; the launch traced here: 83.1 us
  Pallas kernels  77.1 us (93%)
  other arithmetic  4.55 us (5%)
  local copies, waits for them, and re-layouts  1.4 us (2%)
    pallas_call x1, Pallas kernels, local(): pl.pallas_call(kernel, out_shape=jax.ShapeDtypeStruct((vir, vir), F32), i...  77.1 us
    broadcast_in_dim x1, other arithmetic, local(): return updated[None, None]  4.55 us

profile of v2, /device:TPU:1, one launch (start us, length us, event | category | flops | bytes accessed | tf_op | source)
XLA Modules:
  0.0 83.1 jit_solution(12012273223988933187)
XLA Ops:
  0.0 1.4 %fusion.1 = (f32[1]{0:T(128)}, f32[1]{0:T(128)}) fusion(f32[16]{0:T(128)} %param.7, s32[]{:T(128)S(6)} %select_n.6, s32[]{:T(128)S(6)} %select_n.7), kind=kLoop, calls=%fused_computation.2 | loop fusion | bytes 24 | tf_op jit(solution)/shard_map/dynamic_slice | solution.py:334
  1.4 0.0 copy-start
  1.4 0.0 copy-start.1
  1.4 77.1 %doubles_numerator.1 = f32[768,768]{1,0:T(8,128)} custom-call(bf16[144,768]{1,0:T(8,128)(2,1)} %bitcast.10, bf16[768,768]{1,0:T(8,128)(2,1)} %bitcast.9, bf16[768,768]{1,0:T(8,128)(2,1)} %fock.1), custom_call_target="tpu_custom_call" | custom-call | tf_op jit(solution)/shard_map/doubles_numerator/pallas_call | solution.py:304
  78.5 0.0 copy-done
  78.5 0.0 copy-done.1
  78.5 4.6 %fusion = bf16[1,1,768,768]{3,2,1,0:T(8,128)(2,1)} fusion(f32[768,768]{1,0:T(8,128)} %doubles_numerator.1, f32[]{:T(128)} %bitcast.4, f32[]{:T(128)} %bitcast.3, f32[768]{0:T(1024)S(1)} %copy-done.1, bf16[1,1,768,768]{3,2,1,0:T(8,128)(2,1)S(1)} %copy-done), kind=kLoop, calls=%fused_computation.1 | loop fusion | flops 4128768 | bytes 4721672 | tf_op jit(solution)/shard_map/broadcast_in_dim | solution.py:338
Async XLA Ops:
  1.4 77.1 %copy-start = (bf16[1,1,768,768]{3,2,1,0:T(8,128)(2,1)S(1)}, bf16[1,1,768,768]{3,2,1,0:T(8,128)(2,1)}, u32[]{:S(2)}) copy-start(bf16[1,1,768,768]{3,2,1,0:T(8,128)(2,1)} %param.5) | copy-start | bytes 3538948
  1.4 77.1 %copy-start.1 = (f32[768]{0:T(1024)S(1)}, f32[768]{0:T(1024)}, u32[]{:S(2)}) copy-start(f32[768]{0:T(1024)} %param.8) | copy-start | bytes 9220

commit v3 on v2

--- a/solution.py
+++ b/solution.py
@@ -15,30 +15,33 @@
 CHUNKS = (
     (0, 0, 144), (1, 0, 144), (2, 0, 144), (3, 0, 64), (3, 64, 144),
 )
+PIECES = (
+    (0, 0, 144), (1, 0, 144), (2, 0, 144), (3, 0, 64), (3, 64, 144),
+)
 ORDER = (
-    ("start_own", 0, 0), ("load_wait", 0, 0), ("cross", 0, "y"), ("fock", 0, 0), ("y_first", 0, 0),
-    ("z_forward", 1, 0), ("z_forward", 2, 0), ("z_arrive", 1, 0), ("send_y", 1, 0), ("y_second", 0, 0),
-    ("cross", 0, "d"), ("cross", 0, "u"), ("cross", 1, "y"), ("y_opposite", 0, 0), ("cross", 0, "o"),
-    ("y_first", 1, 0), ("merge_core", 0, 0), ("z_forward", 3, 0), ("z_arrive", 2, 0), ("send_y", 2, 0),
-    ("cross", 2, "y"), ("y_second", 1, 0), ("cross", 1, "d"), ("cross", 1, "u"), ("x_relay", 0, 0),
-    ("y_opposite", 1, 0), ("cross", 1, "o"), ("y_first", 2, 0), ("z_arrive", 3, 0), ("send_y", 3, 0),
-    ("cross", 3, "y"), ("merge_core", 1, 0), ("x_done", 0, 0), ("cross", 4, "y"), ("y_second", 2, 0),
-    ("cross", 2, "d"), ("cross", 2, "u"), ("x_relay", 1, 0), ("y_opposite", 2, 0), ("cross", 2, "o"),
-    ("y_first", 3, 0), ("send_y", 4, 0), ("y_second", 3, 0), ("cross", 3, "d"), ("cross", 3, "u"),
-    ("merge_core", 2, 0), ("x_done", 1, 0), ("y_opposite", 3, 0), ("cross", 3, "o"), ("y_first", 4, 0),
-    ("x_relay", 2, 0), ("merge_core", 3, 0), ("y_second", 4, 0), ("cross", 4, "d"), ("cross", 4, "u"),
-    ("y_opposite", 4, 0), ("cross", 4, "o"), ("z_done", 0, 0), ("x_done", 2, 0), ("merge_core", 4, 0),
-    ("x_relay", 3, 0), ("spread", 0, 0), ("x_relay", 4, 0), ("x_done", 3, 0), ("z_done", 1, 0),
-    ("spread_far", 0, 0), ("x_done", 4, 0), ("contract", 0, 0), ("spread", 1, 0), ("z_done", 2, 0),
-    ("spread_far", 1, 0), ("z_done", 3, 0), ("contract", 1, 0), ("spread", 2, 0), ("spread", 3, 0),
-    ("z_done", 4, 0), ("spread_far", 2, 0), ("spread_far", 3, 0), ("spread", 4, 0), ("contract", 2, 0),
-    ("contract", 3, 0), ("spread_far", 4, 0), ("contract", 4, 0),
+    ("start_own", 0, 0), ("load_wait", 0, 0), ("fock", 0, 0), ("y_first", 0, 0), ("z_forward", 1, 0),
+    ("y_second", 0, 0), ("z_forward", 2, 0), ("z_arrive", 1, 0), ("cross", 0, "d"), ("send_y", 1, 0),
+    ("y_opposite", 0, 0), ("cross", 0, "o"), ("cross", 1, "y"), ("cross", 0, "y"), ("cross", 0, "u"),
+    ("y_first", 1, 0), ("z_forward", 3, 0), ("z_arrive", 2, 0), ("merge_core", 0, 0), ("send_y", 2, 0),
+    ("y_second", 1, 0), ("x_relay", 0, 0), ("cross", 1, "d"), ("y_first", 2, 0), ("z_arrive", 3, 0),
+    ("y_opposite", 1, 0), ("cross", 1, "o"), ("cross", 1, "u"), ("x_done", 0, 0), ("cross", 2, "y"),
+    ("merge_core", 1, 0), ("y_second", 2, 0), ("send_y", 3, 0), ("cross", 2, "u"), ("rden", 0, 0),
+    ("cross", 4, "y"), ("y_opposite", 2, 0), ("y_first", 3, 0), ("x_relay", 1, 0), ("cross", 2, "o"),
+    ("cross", 2, "d"), ("cross", 3, "y"), ("merge_core", 2, 0), ("y_second", 3, 0), ("send_y", 4, 0),
+    ("y_opposite", 3, 0), ("z_done", 0, 0), ("cross", 3, "o"), ("cross", 3, "d"), ("x_done", 1, 0),
+    ("y_first", 4, 0), ("x_relay", 2, 0), ("cross", 3, "u"), ("spread", 0, 0), ("merge_core", 3, 0),
+    ("y_opposite", 4, 0), ("cross", 4, "o"), ("y_second", 4, 0), ("cross", 4, "u"), ("cross", 4, "d"),
+    ("x_done", 2, 0), ("merge_core", 4, 0), ("x_relay", 3, 0), ("z_done", 1, 0), ("x_relay", 4, 0),
+    ("x_done", 3, 0), ("spread_far", 0, 0), ("z_done", 2, 0), ("spread", 1, 0), ("x_done", 4, 0),
+    ("z_done", 3, 0), ("spread_far", 1, 0), ("spread", 2, 0), ("contract", 0, 0), ("z_done", 4, 0),
+    ("contract", 1, 0), ("spread", 3, 0), ("spread_far", 2, 0), ("spread", 4, 0), ("spread_far", 3, 0),
+    ("contract", 2, 0), ("spread_far", 4, 0), ("contract", 3, 0), ("contract", 4, 0),
 )
 
 
 def kernel(
-    ints, amp, fock, out,
-    gath, ampv, fockv, acc, temp,
+    ints, amp, fock, eps_occ, eps_vir, out,
+    gath, ampv, fockv, acc, temp, rden, done, occs, virs,
     give, take, part, x1s, x1r, x2s, x2r, zs, zr, dres,
     in_sem, out_sem, send_sem, ra, raz, rcore, rx1, rx2, rz, rd,
 ):
@@ -89,6 +92,8 @@
         pltpu.make_async_copy(amp.at[:, pl.ds(0, half)], ampv.at[0], in_sem.at[1]),
         pltpu.make_async_copy(amp.at[:, pl.ds(half, half)], ampv.at[1], in_sem.at[2]),
         pltpu.make_async_copy(fock, fockv, in_sem.at[3]),
+        pltpu.make_async_copy(eps_occ, occs, in_sem.at[4]),
+        pltpu.make_async_copy(eps_vir, virs, in_sem.at[5]),
     ]
     for load in loads:
         load.start()
@@ -107,16 +112,16 @@
     lo, hi = pl.ds(0, half), pl.ds(half, half)
     is_mine = x * 4 + zh * 2 + p == y * 4 + zl
 
-    def span(i):
-        return CHUNKS[i][1], CHUNKS[i][2]
-
-    def cut(i):
-        a, b = span(i)
+    def span(i, table=CHUNKS):
+        return table[i][1], table[i][2]
+
+    def cut(i, table=CHUNKS):
+        a, b = span(i, table)
         middle = a + ((b - a) // 16 + i % 2) // 2 * 16
         return pl.ds(a, middle - a), pl.ds(middle, b - middle)
 
-    def whole(i):
-        a, b = span(i)
+    def whole(i, table=CHUNKS):
+        a, b = span(i, table)
         return pl.ds(a, b - a)
 
     def block(i, q):
@@ -209,44 +214,47 @@
         arrived(x2r.at[k, 1, whole(i)], rx2.at[i, 1])
         both = x2r[k, 0, a:b].astype(F32) + x2r[k, 1, a:b].astype(F32)
         zs[k, a:b] = (part[k, x, a:b] + both).astype(BF)
-        send(zs.at[k, whole(i)], zr.at[k, whole(i)], rz.at[i], z_far)
+        for c, (of, first, last) in enumerate(PIECES):
+            if of == k and a <= first and last <= b:
+                r = whole(c, PIECES)
+                send(zs.at[k, r], zr.at[k, r], rz.at[c], z_far)
 
     def z_done(i):
-        k, (a, b) = CHUNKS[i][0], span(i)
-        arrived(zr.at[k, whole(i)], rz.at[i])
+        k, (a, b) = PIECES[i][0], span(i, PIECES)
+        arrived(zr.at[k, whole(i, PIECES)], rz.at[i])
         dres[k, p, x, a:b] = (zs[k, a:b].astype(F32) + zr[k, a:b].astype(F32)).astype(BF)
-        b, s = dres.at[k, p, x, whole(i)], rd.at[i, p, x]
+        b, s = dres.at[k, p, x, whole(i, PIECES)], rd.at[i, p, x]
         send(b, b, s.at[0], x_up)
         send(b, b, s.at[0], x_down)
         send(b, b, s.at[0], mate)
 
     def spread(i):
-        k = CHUNKS[i][0]
-        head, tail = cut(i)
+        k = PIECES[i][0]
+        head, tail = cut(i, PIECES)
         for q, piece, sem, where in ((xd, head, 0, x_up), (xu, tail, 1, x_down)):
-            b, s = dres.at[k, p, q, whole(i)], rd.at[i, p, q]
+            b, s = dres.at[k, p, q, whole(i, PIECES)], rd.at[i, p, q]
             arrived(b, s.at[0])
             c = dres.at[k, p, q, piece]
             send(c, c, s.at[sem], where)
             send(b, b, s.at[0], mate)
 
     def spread_far(i):
-        k = CHUNKS[i][0]
-        head, tail = cut(i)
+        k = PIECES[i][0]
+        head, tail = cut(i, PIECES)
         arrived(dres.at[k, p, xo, head], rd.at[i, p, xo, 0])
         arrived(dres.at[k, p, xo, tail], rd.at[i, p, xo, 1])
-        b = dres.at[k, p, xo, whole(i)]
+        b = dres.at[k, p, xo, whole(i, PIECES)]
         send(b, b, rd.at[i, p, xo, 0], mate)
 
     def put(h):
         return pltpu.make_async_copy(
-            acc.at[pl.ds(h * half, half)], out.at[pl.ds(h * half, half)], out_sem.at[h]
+            done.at[pl.ds(h * half, half)], out.at[pl.ds(h * half, half)], out_sem.at[h]
         )
 
     def contract(i):
-        k, (a, b) = CHUNKS[i][0], span(i)
+        k, (a, b) = PIECES[i][0], span(i, PIECES)
         for q in (x, xd, xu, xo):
-            arrived(dres.at[k, 1 - p, q, whole(i)], rd.at[i, 1 - p, q, 0])
+            arrived(dres.at[k, 1 - p, q, whole(i, PIECES)], rd.at[i, 1 - p, q, 0])
         left = gath[rows[k], :, a:b].reshape(4 * (b - a), vir)
         right = jnp.concatenate(
             [dres[k, h, :, a:b].reshape(4 * (b - a), half) for h in range(2)], axis=-1
@@ -254,11 +262,17 @@
         last = ORDER[-1] == ("contract", i, 0)
         for h in range(2):
             r = slice(h * half, (h + 1) * half)
-            acc[r] += lax.dot_general(
+            term = lax.dot_general(
                 left[:, r], right, (((0,), (0,)), ((), ())), preferred_element_type=F32
             )
             if last:
+                change = (acc[r] + term) * rden[r]
+                for c in range(2):
+                    cols = slice(c * half, (c + 1) * half)
+                    done[r, cols] = (ampv[c, r].astype(F32) - change[:, cols]).astype(BF)
                 put(h).start()
+            else:
+                acc[r] += term
 
     def load_wait():
         for load in loads:
@@ -268,6 +282,13 @@
         acc[...] = jnp.dot(ampv[0], fockv[:half], preferred_element_type=F32) + jnp.dot(
             ampv[1], fockv[half:], preferred_element_type=F32
         )
+
+    def denominators():
+        level = occs[x * 4 + zh * 2 + p]
+        level2 = occs[y * 4 + zl]
+        across = virs[...].reshape(1, vir)
+        down = jnp.broadcast_to(across, (128, vir)).T[:, :1]
+        rden[...] = 1.0 / (((down + across) - level) - level2)
 
     for name, i, which in ORDER:
         if name == "cross":
@@ -278,6 +299,8 @@
             load_wait()
         elif name == "fock":
             fock_term()
+        elif name == "rden":
+            denominators()
         else:
             {
                 "z_arrive": z_arrive, "z_forward": z_forward, "send_y": send_y, "y_first": y_first,
@@ -298,13 +321,13 @@
 def local(amplitudes, ints, eps_occ, eps_vir, fock_vir):
     vir, depth = ints.shape[1], ints.shape[2]
     half = vir // 2
-    n = len(CHUNKS)
+    n, n2 = len(CHUNKS), len(PIECES)
     anywhere = pl.BlockSpec(memory_space=pl.ANY)
     dma = pltpu.SemaphoreType.DMA
-    numer = pl.pallas_call(
+    updated = pl.pallas_call(
         kernel,
-        out_shape=jax.ShapeDtypeStruct((vir, vir), F32),
-        in_specs=[anywhere] * 3,
+        out_shape=jax.ShapeDtypeStruct((vir, vir), BF),
+        in_specs=[anywhere] * 5,
         out_specs=anywhere,
         scratch_shapes=[
             pltpu.VMEM((4, 4, depth, vir), BF),
@@ -312,6 +335,10 @@
             pltpu.VMEM((vir, vir), BF),
             pltpu.VMEM((vir, vir), F32),
             pltpu.VMEM((depth, half), F32),
+            pltpu.VMEM((vir, vir), F32),
+            pltpu.VMEM((vir, vir), BF),
+            pltpu.SMEM(eps_occ.shape, F32),
+            pltpu.VMEM((vir,), F32),
             pltpu.VMEM((4, 4, depth, half), BF),
             pltpu.VMEM((4, 4, depth, half), BF),
             pltpu.VMEM((4, 4, depth, half), F32),
@@ -322,19 +349,15 @@
             pltpu.VMEM((4, depth, half), BF),
             pltpu.VMEM((4, depth, half), BF),
             pltpu.VMEM((4, 2, 4, depth, half), BF),
-            dma((4,)), dma((2,)), dma((5 + 23 * n,)),
+            dma((6,)), dma((2,)), dma((5 + 14 * n + 9 * n2,)),
             dma((n, 4, 2)), dma((4,)), dma((n, 4)), dma((n, 2)), dma((n, 2)),
-            dma((n,)), dma((n, 2, 4, 2)),
+            dma((n2,)), dma((n2, 2, 4, 2)),
         ],
         compiler_params=pltpu.CompilerParams(
             collective_id=0, has_side_effects=True, vmem_limit_bytes=60 * 1024 * 1024
         ),
-        name="doubles_numerator",
-    )(ints[0].T, amplitudes[0, 0], fock_vir)
-    level = eps_occ[lax.axis_index(ROW)]
-    level2 = eps_occ[lax.axis_index(COL)]
-    denom = eps_vir[:, None] + eps_vir[None, :] - level - level2
-    updated = (amplitudes[0, 0].astype(F32) - numer / denom).astype(BF)
+        name="doubles_update",
+    )(ints[0].T, amplitudes[0, 0], fock_vir, eps_occ, eps_vir)
     return updated[None, None]
 
 

time: 83.2 us -> 77.7 us (0.934)
  other arithmetic: 4.55 us -> 0 us
  Pallas kernels: 77.1 us -> 75.2 us
  local copies, waits for them, and re-layouts: 1.4 us -> 2.36 us
    broadcast_in_dim x1 -> x0, other arithmetic: 4.55 us -> none  [local(): return updated[None, None]]
    unnamed x4 -> x1, local copies, waits for them, and re-layouts: 0.01 us -> 2.36 us
    pallas_call x1, Pallas kernels: 77.1 us -> 75.2 us  [local(): pl.pallas_call(kernel, out_shape=jax.ShapeDtypeStruct((vir, vir), BF), in...]
    dynamic_slice x1 -> x0, local copies, waits for them, and re-layouts: 1.39 us -> none  [local(): level = eps_occ[lax.axis_index(ROW)]]
where the time goes in v3:
time: 77.7 us; the launch traced here: 77.6 us
  Pallas kernels  75.2 us (97%)
  local copies, waits for them, and re-layouts  2.36 us (3%)
    pallas_call x1, Pallas kernels, local(): pl.pallas_call(kernel, out_shape=jax.ShapeDtypeStruct((vir, vir), BF), in...  75.2 us
    unnamed x1, local copies, waits for them, and re-layouts  2.36 us

profile of v3, /device:TPU:1, one launch (start us, length us, event | category | flops | bytes accessed | tf_op | source)
XLA Modules:
  0.0 77.6 jit_solution(9984581110237552512)
XLA Ops:
  0.0 75.2 %doubles_update.1 = bf16[768,768]{1,0:T(8,128)(2,1)} custom-call(bf16[144,768]{1,0:T(8,128)(2,1)} %bitcast.7, bf16[768,768]{1,0:T(8,128)(2,1)} %bitcast.6, bf16[768,768]{1,0:T(8,128)(2,1)} %fock.1, f32[16]{0:T(128)} %eps_occ.1, f32[768]{0:T(1024)} %eps_vir.1), custom_call_target="tpu_custom_call" | custom-call | tf_op jit(solution)/shard_map/doubles_update/pallas_call | solution.py:327
  75.2 2.4 %copy.7 = bf16[1,1,768,768]{3,2,1,0:T(8,128)(2,1)} copy(bf16[1,1,768,768]{3,2,1,0:T(8,128)(2,1)} %bitcast.5) | data formatting | bytes 2359296

commit v4 on v3

--- a/solution.py
+++ b/solution.py
@@ -13,29 +13,26 @@
 F32 = jnp.float32
 
 CHUNKS = (
-    (0, 0, 144), (1, 0, 144), (2, 0, 144), (3, 0, 64), (3, 64, 144),
+    (0, 0, 144), (1, 0, 144), (2, 0, 144), (3, 0, 144),
 )
 PIECES = (
-    (0, 0, 144), (1, 0, 144), (2, 0, 144), (3, 0, 64), (3, 64, 144),
+    (0, 0, 144), (1, 0, 144), (2, 0, 144), (3, 0, 144),
 )
 ORDER = (
-    ("start_own", 0, 0), ("load_wait", 0, 0), ("fock", 0, 0), ("y_first", 0, 0), ("z_forward", 1, 0),
-    ("y_second", 0, 0), ("z_forward", 2, 0), ("z_arrive", 1, 0), ("cross", 0, "d"), ("send_y", 1, 0),
-    ("y_opposite", 0, 0), ("cross", 0, "o"), ("cross", 1, "y"), ("cross", 0, "y"), ("cross", 0, "u"),
-    ("y_first", 1, 0), ("z_forward", 3, 0), ("z_arrive", 2, 0), ("merge_core", 0, 0), ("send_y", 2, 0),
-    ("y_second", 1, 0), ("x_relay", 0, 0), ("cross", 1, "d"), ("y_first", 2, 0), ("z_arrive", 3, 0),
-    ("y_opposite", 1, 0), ("cross", 1, "o"), ("cross", 1, "u"), ("x_done", 0, 0), ("cross", 2, "y"),
-    ("merge_core", 1, 0), ("y_second", 2, 0), ("send_y", 3, 0), ("cross", 2, "u"), ("rden", 0, 0),
-    ("cross", 4, "y"), ("y_opposite", 2, 0), ("y_first", 3, 0), ("x_relay", 1, 0), ("cross", 2, "o"),
-    ("cross", 2, "d"), ("cross", 3, "y"), ("merge_core", 2, 0), ("y_second", 3, 0), ("send_y", 4, 0),
-    ("y_opposite", 3, 0), ("z_done", 0, 0), ("cross", 3, "o"), ("cross", 3, "d"), ("x_done", 1, 0),
-    ("y_first", 4, 0), ("x_relay", 2, 0), ("cross", 3, "u"), ("spread", 0, 0), ("merge_core", 3, 0),
-    ("y_opposite", 4, 0), ("cross", 4, "o"), ("y_second", 4, 0), ("cross", 4, "u"), ("cross", 4, "d"),
-    ("x_done", 2, 0), ("merge_core", 4, 0), ("x_relay", 3, 0), ("z_done", 1, 0), ("x_relay", 4, 0),
-    ("x_done", 3, 0), ("spread_far", 0, 0), ("z_done", 2, 0), ("spread", 1, 0), ("x_done", 4, 0),
-    ("z_done", 3, 0), ("spread_far", 1, 0), ("spread", 2, 0), ("contract", 0, 0), ("z_done", 4, 0),
-    ("contract", 1, 0), ("spread", 3, 0), ("spread_far", 2, 0), ("spread", 4, 0), ("spread_far", 3, 0),
-    ("contract", 2, 0), ("spread_far", 4, 0), ("contract", 3, 0), ("contract", 4, 0),
+    ("start_own", 0, 0), ("y_first", 0, 0), ("z_forward", 1, 0), ("load_wait", 0, 0), ("cross", 0, "y"),
+    ("z_arrive", 1, 0), ("z_forward", 2, 0), ("send_y", 1, 0), ("cross", 1, "y"), ("fock", 0, 0),
+    ("y_first", 1, 0), ("z_arrive", 2, 0), ("y_opposite", 0, 0), ("cross", 0, "o"), ("y_second", 1, 0),
+    ("y_second", 0, 0), ("z_forward", 3, 0), ("send_y", 2, 0), ("cross", 1, "u"), ("cross", 0, "d"),
+    ("cross", 0, "u"), ("cross", 1, "d"), ("merge_core", 0, 0), ("y_opposite", 1, 0), ("cross", 1, "o"),
+    ("y_first", 2, 0), ("z_arrive", 3, 0), ("x_relay", 0, 0), ("y_second", 2, 0), ("cross", 2, "d"),
+    ("merge_core", 1, 0), ("cross", 2, "y"), ("send_y", 3, 0), ("y_opposite", 2, 0), ("cross", 2, "o"),
+    ("x_relay", 1, 0), ("cross", 2, "u"), ("x_done", 0, 0), ("y_first", 3, 0), ("merge_core", 2, 0),
+    ("y_second", 3, 0), ("cross", 3, "d"), ("cross", 3, "y"), ("cross", 3, "u"), ("x_done", 1, 0),
+    ("x_relay", 2, 0), ("y_opposite", 3, 0), ("cross", 3, "o"), ("merge_core", 3, 0), ("rden", 0, 0),
+    ("z_done", 0, 0), ("x_done", 2, 0), ("x_relay", 3, 0), ("spread", 0, 0), ("z_done", 1, 0),
+    ("x_done", 3, 0), ("z_done", 2, 0), ("spread_far", 0, 0), ("spread", 1, 0), ("z_done", 3, 0),
+    ("contract", 0, 0), ("spread_far", 1, 0), ("spread", 2, 0), ("spread", 3, 0), ("contract", 1, 0),
+    ("spread_far", 2, 0), ("spread_far", 3, 0), ("contract", 2, 0), ("contract", 3, 0),
 )
 
 

time: 77.7 us -> 75.7 us (0.974)
  Pallas kernels: 75.2 us -> 73.2 us
    pallas_call x1, Pallas kernels: 75.2 us -> 73.2 us  [local(): pl.pallas_call(kernel, out_shape=jax.ShapeDtypeStruct((vir, vir), BF), in...]
where the time goes in v4:
time: 75.7 us; the launch traced here: 75.5 us
  Pallas kernels  73.2 us (97%)
  local copies, waits for them, and re-layouts  2.36 us (3%)
    pallas_call x1, Pallas kernels, local(): pl.pallas_call(kernel, out_shape=jax.ShapeDtypeStruct((vir, vir), BF), in...  73.2 us
    unnamed x1, local copies, waits for them, and re-layouts  2.36 us

profile of v4, /device:TPU:1, one launch (start us, length us, event | category | flops | bytes accessed | tf_op | source)
XLA Modules:
  0.0 75.5 jit_solution(13711985422221049740)
XLA Ops:
  0.0 73.2 %doubles_update.1 = bf16[768,768]{1,0:T(8,128)(2,1)} custom-call(bf16[144,768]{1,0:T(8,128)(2,1)} %bitcast.7, bf16[768,768]{1,0:T(8,128)(2,1)} %bitcast.6, bf16[768,768]{1,0:T(8,128)(2,1)} %fock.1, f32[16]{0:T(128)} %eps_occ.1, f32[768]{0:T(1024)} %eps_vir.1), custom_call_target="tpu_custom_call" | custom-call | tf_op jit(solution)/shard_map/doubles_update/pallas_call | solution.py:324
  73.2 2.4 %copy.7 = bf16[1,1,768,768]{3,2,1,0:T(8,128)(2,1)} copy(bf16[1,1,768,768]{3,2,1,0:T(8,128)(2,1)} %bitcast.5) | data formatting | bytes 2359296

commit v5 on v4

--- a/solution.py
+++ b/solution.py
@@ -16,23 +16,24 @@
     (0, 0, 144), (1, 0, 144), (2, 0, 144), (3, 0, 144),
 )
 PIECES = (
-    (0, 0, 144), (1, 0, 144), (2, 0, 144), (3, 0, 144),
+    (0, 0, 144), (1, 0, 144), (2, 0, 144), (3, 0, 64), (3, 64, 144),
 )
 ORDER = (
-    ("start_own", 0, 0), ("y_first", 0, 0), ("z_forward", 1, 0), ("load_wait", 0, 0), ("cross", 0, "y"),
-    ("z_arrive", 1, 0), ("z_forward", 2, 0), ("send_y", 1, 0), ("cross", 1, "y"), ("fock", 0, 0),
-    ("y_first", 1, 0), ("z_arrive", 2, 0), ("y_opposite", 0, 0), ("cross", 0, "o"), ("y_second", 1, 0),
-    ("y_second", 0, 0), ("z_forward", 3, 0), ("send_y", 2, 0), ("cross", 1, "u"), ("cross", 0, "d"),
-    ("cross", 0, "u"), ("cross", 1, "d"), ("merge_core", 0, 0), ("y_opposite", 1, 0), ("cross", 1, "o"),
-    ("y_first", 2, 0), ("z_arrive", 3, 0), ("x_relay", 0, 0), ("y_second", 2, 0), ("cross", 2, "d"),
-    ("merge_core", 1, 0), ("cross", 2, "y"), ("send_y", 3, 0), ("y_opposite", 2, 0), ("cross", 2, "o"),
-    ("x_relay", 1, 0), ("cross", 2, "u"), ("x_done", 0, 0), ("y_first", 3, 0), ("merge_core", 2, 0),
-    ("y_second", 3, 0), ("cross", 3, "d"), ("cross", 3, "y"), ("cross", 3, "u"), ("x_done", 1, 0),
-    ("x_relay", 2, 0), ("y_opposite", 3, 0), ("cross", 3, "o"), ("merge_core", 3, 0), ("rden", 0, 0),
-    ("z_done", 0, 0), ("x_done", 2, 0), ("x_relay", 3, 0), ("spread", 0, 0), ("z_done", 1, 0),
-    ("x_done", 3, 0), ("z_done", 2, 0), ("spread_far", 0, 0), ("spread", 1, 0), ("z_done", 3, 0),
-    ("contract", 0, 0), ("spread_far", 1, 0), ("spread", 2, 0), ("spread", 3, 0), ("contract", 1, 0),
-    ("spread_far", 2, 0), ("spread_far", 3, 0), ("contract", 2, 0), ("contract", 3, 0),
+    ("start_own", 0, 0), ("y_first", 0, 0), ("z_forward", 1, 0), ("z_arrive", 1, 0), ("send_y", 1, 0),
+    ("z_forward", 2, 0), ("y_second", 0, 0), ("load_wait", 0, 0), ("cross", 0, "y"), ("cross", 0, "u"),
+    ("cross", 0, "d"), ("z_forward", 3, 0), ("y_opposite", 0, 0), ("cross", 1, "y"), ("cross", 0, "o"),
+    ("y_first", 1, 0), ("z_arrive", 2, 0), ("send_y", 2, 0), ("merge_core", 0, 0), ("y_second", 1, 0),
+    ("cross", 1, "u"), ("fock", 0, 0), ("cross", 1, "d"), ("x_relay", 0, 0), ("y_opposite", 1, 0),
+    ("cross", 1, "o"), ("y_first", 2, 0), ("merge_core", 1, 0), ("cross", 2, "y"), ("x_done", 0, 0),
+    ("z_arrive", 3, 0), ("send_y", 3, 0), ("cross", 3, "y"), ("y_second", 2, 0), ("cross", 2, "d"),
+    ("rden", 0, 0), ("cross", 2, "u"), ("x_relay", 1, 0), ("y_opposite", 2, 0), ("cross", 2, "o"),
+    ("merge_core", 2, 0), ("y_first", 3, 0), ("z_done", 0, 0), ("x_done", 1, 0), ("y_second", 3, 0),
+    ("x_relay", 2, 0), ("cross", 3, "d"), ("cross", 3, "u"), ("y_opposite", 3, 0), ("cross", 3, "o"),
+    ("merge_core", 3, 0), ("x_done", 2, 0), ("spread", 0, 0), ("x_relay", 3, 0), ("spread_far", 0, 0),
+    ("z_done", 1, 0), ("x_done", 3, 0), ("z_done", 2, 0), ("spread", 1, 0), ("contract", 0, 0),
+    ("spread", 2, 0), ("z_done", 3, 0), ("z_done", 4, 0), ("spread_far", 1, 0), ("spread", 3, 0),
+    ("spread_far", 2, 0), ("spread", 4, 0), ("contract", 1, 0), ("spread_far", 3, 0), ("contract", 4, 1),
+    ("spread_far", 4, 0), ("contract", 2, 0), ("contract", 3, 0), ("contract", 4, 2),
 )
 
 
@@ -248,15 +249,21 @@
             done.at[pl.ds(h * half, half)], out.at[pl.ds(h * half, half)], out_sem.at[h]
         )
 
-    def contract(i):
+    def contract(i, part):
         k, (a, b) = PIECES[i][0], span(i, PIECES)
-        for q in (x, xd, xu, xo):
+        order = ((x, xd, xu, xo), (x, xd, xu), (xo,))[part]
+        for q in order:
             arrived(dres.at[k, 1 - p, q, whole(i, PIECES)], rd.at[i, 1 - p, q, 0])
-        left = gath[rows[k], :, a:b].reshape(4 * (b - a), vir)
-        right = jnp.concatenate(
-            [dres[k, h, :, a:b].reshape(4 * (b - a), half) for h in range(2)], axis=-1
-        )
-        last = ORDER[-1] == ("contract", i, 0)
+        if part == 0:
+            left = gath[rows[k], :, a:b].reshape(4 * (b - a), vir)
+            sides = [dres[k, h, :, a:b].reshape(4 * (b - a), half) for h in range(2)]
+        else:
+            left = jnp.concatenate([gath[rows[k], q, a:b] for q in order], axis=0)
+            sides = [
+                jnp.concatenate([dres[k, h, q, a:b] for q in order], axis=0) for h in range(2)
+            ]
+        right = jnp.concatenate(sides, axis=-1)
+        last = ORDER[-1] == ("contract", i, part)
         for h in range(2):
             r = slice(h * half, (h + 1) * half)
             term = lax.dot_general(
@@ -290,6 +297,8 @@
     for name, i, which in ORDER:
         if name == "cross":
             cross(i, which)
+        elif name == "contract":
+            contract(i, which)
         elif name == "start_own":
             start_own()
         elif name == "load_wait":
@@ -303,7 +312,7 @@
                 "z_arrive": z_arrive, "z_forward": z_forward, "send_y": send_y, "y_first": y_first,
                 "y_second": y_second, "y_opposite": y_opposite, "merge_core": merge_core,
                 "x_relay": x_relay, "x_done": x_done, "z_done": z_done, "spread": spread,
-                "spread_far": spread_far, "contract": contract,
+                "spread_far": spread_far,
             }[name](i)
 
     for copy, guard in started:

time: 75.7 us -> 75 us (level)
  no operation moved by 1% of the time
where the time goes in v5:
time: 75 us; the launch traced here: 74.8 us
  Pallas kernels  72.5 us (97%)
  local copies, waits for them, and re-layouts  2.36 us (3%)
    pallas_call x1, Pallas kernels, local(): pl.pallas_call(kernel, out_shape=jax.ShapeDtypeStruct((vir, vir), BF), in...  72.5 us
    unnamed x1, local copies, waits for them, and re-layouts  2.36 us

profile of v5, /device:TPU:1, one launch (start us, length us, event | category | flops | bytes accessed | tf_op | source)
XLA Modules:
  0.0 74.8 jit_solution(7144488590223058828)
XLA Ops:
  0.0 72.5 %doubles_update.1 = bf16[768,768]{1,0:T(8,128)(2,1)} custom-call(bf16[144,768]{1,0:T(8,128)(2,1)} %bitcast.7, bf16[768,768]{1,0:T(8,128)(2,1)} %bitcast.6, bf16[768,768]{1,0:T(8,128)(2,1)} %fock.1, f32[16]{0:T(128)} %eps_occ.1, f32[768]{0:T(1024)} %eps_vir.1), custom_call_target="tpu_custom_call" | custom-call | tf_op jit(solution)/shard_map/doubles_update/pallas_call | solution.py:333
  72.5 2.4 %copy.7 = bf16[1,1,768,768]{3,2,1,0:T(8,128)(2,1)} copy(bf16[1,1,768,768]{3,2,1,0:T(8,128)(2,1)} %bitcast.5) | data formatting | bytes 2359296

commit v6 on v5

--- a/solution.py
+++ b/solution.py
@@ -44,7 +44,7 @@
     in_sem, out_sem, send_sem, ra, raz, rcore, rx1, rx2, rz, rd,
 ):
     vir = ints.shape[1]
-    half = vir // 2
+    half, third = vir // 2, vir // 3
     x, zh, p = lax.axis_index("x"), lax.axis_index("zh"), lax.axis_index("core")
     y, zl = lax.axis_index("y"), lax.axis_index("zl")
     side = zl // 2
@@ -246,7 +246,7 @@
 
     def put(h):
         return pltpu.make_async_copy(
-            done.at[pl.ds(h * half, half)], out.at[pl.ds(h * half, half)], out_sem.at[h]
+            done.at[pl.ds(h * third, third)], out.at[pl.ds(h * third, third)], out_sem.at[h]
         )
 
     def contract(i, part):
@@ -264,8 +264,8 @@
             ]
         right = jnp.concatenate(sides, axis=-1)
         last = ORDER[-1] == ("contract", i, part)
-        for h in range(2):
-            r = slice(h * half, (h + 1) * half)
+        for h in range(3):
+            r = slice(h * third, (h + 1) * third)
             term = lax.dot_general(
                 left[:, r], right, (((0,), (0,)), ((), ())), preferred_element_type=F32
             )
@@ -320,7 +320,7 @@
             copy.wait_send()
         else:
             pl.when(guard)(copy.wait_send)
-    for h in range(2):
+    for h in range(3):
         put(h).wait()
 
 
@@ -355,7 +355,7 @@
             pltpu.VMEM((4, depth, half), BF),
             pltpu.VMEM((4, depth, half), BF),
             pltpu.VMEM((4, 2, 4, depth, half), BF),
-            dma((6,)), dma((2,)), dma((5 + 14 * n + 9 * n2,)),
+            dma((6,)), dma((3,)), dma((5 + 14 * n + 9 * n2,)),
             dma((n, 4, 2)), dma((4,)), dma((n, 4)), dma((n, 2)), dma((n, 2)),
             dma((n2,)), dma((n2, 2, 4, 2)),
         ],

time: 75 us -> 75 us (level)
  no operation moved by 1% of the time
where the time goes in v6:
time: 75 us; the launch traced here: 74.9 us
  Pallas kernels  72.5 us (97%)
  local copies, waits for them, and re-layouts  2.36 us (3%)
    pallas_call x1, Pallas kernels, local(): pl.pallas_call(kernel, out_shape=jax.ShapeDtypeStruct((vir, vir), BF), in...  72.5 us
    unnamed x1, local copies, waits for them, and re-layouts  2.36 us

profile of v6, /device:TPU:1, one launch (start us, length us, event | category | flops | bytes accessed | tf_op | source)
XLA Modules:
  0.0 74.9 jit_solution(17663268958373605963)
XLA Ops:
  0.0 72.5 %doubles_update.1 = bf16[768,768]{1,0:T(8,128)(2,1)} custom-call(bf16[144,768]{1,0:T(8,128)(2,1)} %bitcast.7, bf16[768,768]{1,0:T(8,128)(2,1)} %bitcast.6, bf16[768,768]{1,0:T(8,128)(2,1)} %fock.1, f32[16]{0:T(128)} %eps_occ.1, f32[768]{0:T(1024)} %eps_vir.1), custom_call_target="tpu_custom_call" | custom-call | tf_op jit(solution)/shard_map/doubles_update/pallas_call | solution.py:333
  72.5 2.4 %copy.7 = bf16[1,1,768,768]{3,2,1,0:T(8,128)(2,1)} copy(bf16[1,1,768,768]{3,2,1,0:T(8,128)(2,1)} %bitcast.5) | data formatting | bytes 2359296
